TPU v7x, 32 devices: a whole 2x2x4 slice. The times are simulated.
32 devices in a mesh: layer: 16 (over z, y, core), dp: 2 (over x).
Axes of the slice: x: 2, y: 2, z: 4, core: 2. Of those that a mesh axis runs over, the one named last changes fastest.
Arguments:
- c_guess: float32 [16, 256, 512], P('layer', 'dp'), may hold values from -6 to 6
- adj_guess: float32 [16, 256, 512], P('layer', 'dp'), may hold values from -6 to 6
- norm_gain: float32 [32, 512], P('layer'), may hold values from 0.5 to 1.5
- w_up: bfloat16 [32, 512, 2048], P('layer'), may hold values from -0.25 to 0.25
- w_down: bfloat16 [32, 2048, 512], P('layer'), may hold values from -0.125 to 0.125
- coarse_rate: float32 [16, 512], P('layer'), may hold values from 0.5 to 1
Outputs:
- c_points: float32 [16, 256, 512], P('layer', 'dp')
- adj_points: float32 [16, 256, 512], P('layer', 'dp')
- grad_up: float32 [32, 512, 2048], P('layer', 'dp')
- grad_down: float32 [32, 2048, 512], P('layer', 'dp')
All inputs are finite; a program needn't handle non-finite values.
Results may differ from a plain program's by a relative error of at most 0.018.
Values may be sent and summed in bfloat16 or wider, within the bound.
A program may use at most 64 MiB of HBM per device.

v0:
```python
import jax
import jax.numpy as jnp
from jax import lax
from jax.sharding import PartitionSpec as P

eps = 1e-06
step_length = 0.5


def carried_in(x, axis, combine, identity, reverse):
    size, here = (lax.axis_size(axis), lax.axis_index(axis))
    everything = jax.tree.map(lambda part: lax.all_gather(part, axis), x)
    start = jax.tree.map(
        lambda part, zero: jnp.broadcast_to(jnp.asarray(zero, part.dtype), part.shape), x, identity
    )

    def step(k, before):
        at = size - 1 - k if reverse else k
        reached = at > here if reverse else at < here
        new = combine(before, jax.tree.map(lambda part: part[at], everything))
        return jax.tree.map(lambda a, b: jnp.where(reached, a, b), new, before)

    return lax.fori_loop(0, size, step, start)


def normalize(state):
    inverse_rms = lax.rsqrt(jnp.mean(state * state, axis=-1, keepdims=True) + eps)
    return (state * inverse_rms, inverse_rms)


def layer_forward(state, gain_row, up_matrix, down_matrix):
    unit_state, inverse_rms = normalize(state)
    normed = (unit_state * gain_row).astype(jnp.bfloat16)
    preact = jnp.dot(normed, up_matrix, preferred_element_type=jnp.float32)
    hidden = jax.nn.silu(preact).astype(jnp.bfloat16)
    return state + step_length * jnp.dot(hidden, down_matrix, preferred_element_type=jnp.float32)


def layer_backward(state, cotangent, gain_row, up_matrix, down_matrix):
    unit_state, inverse_rms = normalize(state)
    normed = (unit_state * gain_row).astype(jnp.bfloat16)
    preact = jnp.dot(normed, up_matrix, preferred_element_type=jnp.float32)
    hidden = jax.nn.silu(preact).astype(jnp.bfloat16)
    sigmoid_pre = jax.nn.sigmoid(preact)
    out_grad = (step_length * cotangent).astype(jnp.bfloat16)
    hidden_grad = jnp.dot(out_grad, down_matrix.T, preferred_element_type=jnp.float32)
    pre_grad = (hidden_grad * sigmoid_pre * (1.0 + preact * (1.0 - sigmoid_pre))).astype(
        jnp.bfloat16
    )
    normed_grad = jnp.dot(pre_grad, up_matrix.T, preferred_element_type=jnp.float32)
    unit_grad = normed_grad * gain_row
    inner = jnp.mean(unit_grad * unit_state, axis=-1, keepdims=True)
    new_cotangent = cotangent + inverse_rms * (unit_grad - unit_state * inner)
    return (new_cotangent, normed, pre_grad, hidden, out_grad)


def block_forward(state, gains, ups, downs):
    for depth_index in range(gains.shape[0]):
        state = layer_forward(state, gains[depth_index], ups[depth_index], downs[depth_index])
    return state


def block_inputs(state, gains, ups, downs):
    inputs = [state]
    state = layer_forward(state, gains[0], ups[0], downs[0])
    inputs.append(state)
    return inputs


def block_backward(inputs, cotangent, gains, ups, downs):
    normed_list, pre_list, hidden_list, out_list = ([], [], [], [])
    for depth_index in reversed(range(gains.shape[0])):
        cotangent, normed, pre_grad, hidden, out_grad = layer_backward(
            inputs[depth_index], cotangent, gains[depth_index], ups[depth_index], downs[depth_index]
        )
        normed_list.insert(0, normed)
        pre_list.insert(0, pre_grad)
        hidden_list.insert(0, hidden)
        out_list.insert(0, out_grad)
    factors = (
        jnp.stack(normed_list),
        jnp.stack(pre_list),
        jnp.stack(hidden_list),
        jnp.stack(out_list),
    )
    return (cotangent, factors)


def compose(earlier, later):
    return (earlier[0] * later[0], later[0] * earlier[1] + later[1])


def shards(c_guess, adj_guess, norm_gain, w_up, w_down, coarse_rate):
    position = lax.axis_index("layer")
    devices = lax.axis_size("layer")
    leading = position == 0
    trailing = position == devices - 1
    start_state = c_guess[0]
    decay_rate = coarse_rate[0]
    identity_map = (jnp.ones_like(decay_rate), jnp.zeros_like(start_state))
    block_end = block_forward(start_state, norm_gain, w_up, w_down)
    forward_rate = jnp.where(leading, jnp.zeros_like(decay_rate), decay_rate)
    forward_shift = block_end - forward_rate * start_state
    _, carried = carried_in((forward_rate, forward_shift), "layer", compose, identity_map, False)
    point = jnp.where(leading, start_state, carried)
    inputs = block_inputs(point, norm_gain, w_up, w_down)
    adjoint_guess = adj_guess[0]
    begin, _ = block_backward(inputs, adjoint_guess, norm_gain, w_up, w_down)
    backward_rate = jnp.where(trailing, jnp.zeros_like(decay_rate), decay_rate)
    backward_shift = begin - backward_rate * adjoint_guess
    _, carried_back = carried_in(
        (backward_rate, backward_shift), "layer", compose, identity_map, True
    )
    adjoint = jnp.where(trailing, adjoint_guess, carried_back)
    _, factors = block_backward(inputs, adjoint, norm_gain, w_up, w_down)
    normed_all, pre_all, hidden_all, out_all = factors
    group = lax.axis_size("dp")
    member = lax.axis_index("dp")
    width_share = w_up.shape[1] // group
    hidden_share = w_up.shape[2] // group
    piece_normed = lax.all_gather(normed_all, "dp", axis=1, tiled=True)
    piece_pre = lax.all_gather(pre_all, "dp", axis=1, tiled=True)
    piece_hidden = lax.all_gather(hidden_all, "dp", axis=1, tiled=True)
    piece_out = lax.all_gather(out_all, "dp", axis=1, tiled=True)
    normed_cols = lax.dynamic_slice_in_dim(piece_normed, member * width_share, width_share, 2)
    hidden_cols = lax.dynamic_slice_in_dim(piece_hidden, member * hidden_share, hidden_share, 2)
    up_part = jnp.einsum("ltd,ltf->ldf", normed_cols, piece_pre, preferred_element_type=jnp.float32)
    down_part = jnp.einsum(
        "ltf,ltd->lfd", hidden_cols, piece_out, preferred_element_type=jnp.float32
    )
    return (point[None], adjoint[None], up_part, down_part)


def solution(mesh):
    return jax.shard_map(
        shards,
        mesh=mesh,
        in_specs=(
            P("layer", "dp", None),
            P("layer", "dp", None),
            P("layer", None),
            P("layer", None, None),
            P("layer", None, None),
            P("layer", None),
        ),
        out_specs=(
            P("layer", "dp", None),
            P("layer", "dp", None),
            P("layer", "dp", None),
            P("layer", "dp", None),
        ),
        check_vma=False,
    )
```

profile of v0, /device:TPU:0, one launch (start us, length us, event | category | flops | bytes accessed | tf_op | source)
XLA Modules:
  0.0 239.0 jit_solution(10892800529612794329)
XLA Ops:
  9.1 3.2 %multiply_reduce_fusion.5 = (f32[128]{0:T(128)S(1)}, f32[128,512]{1,0:T(8,128)S(1)}) fusion(bf16[2,2048,512]{2,1,0:T(8,128)(2,1)} %param.14, bf16[2,512,2048]{2,1,0:T(8,128)(2,1)} %param.13, f32[1,128,512]{2,1,0:T(8,128)} %param.10, f32[512]{0:T(512)S(1)} %bitcast.178, f32[128]{0:T(128)S(1)} %add_rsqrt_fusion.3), kind=kOutput, calls=%fused_computation.108 | convolution fusion | flops 538640256 | bytes 4983808 | tf_op jit(solution)/shard_map/dot_general | solution.py:36
  12.3 3.7 %fusion.76 = f32[128,512]{1,0:T(8,128)} fusion(f32[128,512]{1,0:T(8,128)S(1)} %get-tuple-element.301, bf16[2,2048,512]{2,1,0:T(8,128)(2,1)} %param.14, bf16[2,512,2048]{2,1,0:T(8,128)(2,1)} %param.13, f32[1,128,512]{2,1,0:T(8,128)S(1)} %copy-done.3, f32[512]{0:T(512)S(1)} %bitcast.184, f32[512]{0:T(512)S(1)} %bitcast.173, f32[128]{0:T(128)S(1)} %add_rsqrt_fusion.2), kind=kOutput, calls=%fused_computation.66 | convolution fusion | flops 538640384 | bytes 5247488 | tf_op jit(solution)/shard_map/dot_general | solution.py:36
  16.1 23.3 %all-gather.2 = f32[16,1,512]{2,1,0:T(1,128)S(1)} all-gather(f32[1,1,512]{2,1,0:T(1,128)S(1)} %bitcast.185), channel_id=1, replica_groups=mesh['layer'=16,'dp'=2] {'layer'}, dimensions={0}, use_global_device_ids=true | all-gather | bytes 34816 | tf_op jit(solution)/shard_map/all_gather | solution.py:12
  39.4 29.9 %all-gather.13.cloned.1.call-done = f32[2048,512]{1,0:T(8,128)} async-done(((f32[128,512]{1,0:T(8,128)}), f32[2048,512]{1,0:T(8,128)}) %all-gather.13.cloned.1.call-update) | async-done | bytes 4194320 | tf_op jit(solution)/shard_map/all_gather | solution.py:12
  69.3 19.1 %while.30 = (s32[]{:T(128)}, f32[128,512]{1,0:T(8,128)S(1)}, s32[]{:T(128)}, f32[16,512]{1,0:T(8,128)S(1)}, f32[16,128,512]{2,1,0:T(8,128)}, /*index=5*/s32[]{:T(128)}, s32[]{:T(128)}) while((s32[]{:T(128)}, f32[128,512]{1,0:T(8,128)S(1)}, s32[]{:T(128)}, f32[16,512]{1,0:T(8,128)S(1)}, f32[16,128,512]{2,1,0:T(8,128)}, ...), condition=%wide.region_3.4_spmd.clone, body=%wide.region_2.3_spmd.clone.sunk | while | flops 262148 | bytes 792689 | solution.py:23
  70.5 1.2 fusion.150
  71.7 1.2 fusion.150
  74.1 1.2 fusion.150
  75.3 1.2 fusion.150
  77.7 1.2 fusion.150
  78.9 1.2 fusion.150
  80.1 1.2 fusion.150
  81.3 1.2 fusion.150
  83.7 1.2 fusion.150
  88.6 2.2 fusion.31
  92.0 1.5 copy-done.1
  94.1 4.5 %multiply_reduce_fusion.2 = (f32[128]{0:T(128)S(1)}, f32[128,512]{1,0:T(8,128)}) fusion(f32[128,512]{1,0:T(8,128)S(1)} %get-tuple-element.303, f32[128]{0:T(128)S(1)} %add_rsqrt_fusion, f32[512]{0:T(512)S(1)} %bitcast.175, bf16[2,512,2048]{2,1,0:T(8,128)(2,1)} %param.13, bf16[2,2048,512]{2,1,0:T(8,128)(2,1)} %param.14, f32[128,2048]{1,0:T(8,128)S(1)} %fusion.19, ...), kind=kOutput, calls=%fused_computation.101 | convolution fusion | flops 539623296 | bytes 6032384 | tf_op jit(solution)/shard_map/dot_general | solution.py:50
  98.6 3.9 %fusion.49 = f32[128,512]{1,0:T(8,128)S(1)} fusion(bf16[2,512,2048]{2,1,0:T(8,128)(2,1)} %param.13, bf16[2,2048,512]{2,1,0:T(8,128)(2,1)} %param.14, f32[128,2048]{1,0:T(8,128)S(1)} %fusion.31, f32[512]{0:T(512)S(1)} %bitcast.180, f32[1,128,512]{2,1,0:T(8,128)S(1)} %copy-done.4, f32[128,512]{1,0:T(8,128)} %get-tuple-element.305, ...), kind=kOutput, calls=%fused_computation.57 | convolution fusion | flops 539754496 | bytes 6294528 | tf_op jit(solution)/shard_map/dot_general | solution.py:50
  102.7 1.8 fusion.133
  104.6 19.1 %all-gather.3 = f32[16,1,512]{2,1,0:T(1,128)S(1)} all-gather(f32[1,1,512]{2,1,0:T(1,128)S(1)} %bitcast.183), channel_id=1, replica_groups=mesh['layer'=16,'dp'=2] {'layer'}, dimensions={0}, use_global_device_ids=true | all-gather | bytes 34816 | tf_op jit(solution)/shard_map/all_gather | solution.py:12
  125.4 28.2 %all-gather.15.cloned.1.call-done = f32[2048,512]{1,0:T(8,128)} async-done(((f32[128,512]{1,0:T(8,128)}), f32[2048,512]{1,0:T(8,128)}) %all-gather.15.cloned.1.call-update) | async-done | bytes 4194320 | tf_op jit(solution)/shard_map/all_gather | solution.py:12
  153.7 19.3 %while.31 = (s32[]{:T(128)}, f32[128,512]{1,0:T(8,128)S(1)}, s32[]{:T(128)}, f32[16,512]{1,0:T(8,128)S(1)}, f32[16,128,512]{2,1,0:T(8,128)}, /*index=5*/s32[]{:T(128)}, s32[]{:T(128)}, s32[]{:T(128)}, s32[]{:T(128)}) while((s32[]{:T(128)}, f32[128,512]{1,0:T(8,128)S(1)}, s32[]{:T(128)}, f32[16,512]{1,0:T(8,128)S(1)}, ...), condition=%wide.region_9.10_spmd.clone, body=%wide.region_8.9_spmd.clone.sunk | while | flops 262152 | bytes 792751 | solution.py:23
  159.7 1.2 fusion.151
  160.9 1.2 fusion.151
  162.1 1.2 fusion.151
  163.3 1.2 fusion.151
  173.0 2.6 %fusion.8 = bf16[128,2048]{1,0:T(8,128)(2,1)S(1)} fusion(bf16[2,2048,512]{2,1,0:T(8,128)(2,1)} %param.14, f32[128,2048]{1,0:T(8,128)S(1)} %fusion.19, f32[128,512]{1,0:T(8,128)S(1)} %get-tuple-element.289), kind=kOutput, calls=%fused_computation.16 | convolution fusion | flops 270925824 | bytes 3932160 | tf_op jit(solution)/shard_map/dot_general | solution.py:46
  180.2 12.6 %all_gather.38 = bf16[2,256,512]{2,1,0:T(8,128)(2,1)S(1)} all-gather(bf16[2,128,512]{2,1,0:T(8,128)(2,1)S(1)} %pad_maximum_fusion.2), channel_id=1, replica_groups=mesh['layer'=16,'dp'=2] {'dp'}, dimensions={1}, use_global_device_ids=true | all-gather | bytes 786432 | tf_op jit(solution)/shard_map/all_gather | solution.py:121
  192.8 8.8 %all_gather.41 = bf16[2,256,512]{2,1,0:T(8,128)(2,1)S(1)} all-gather(bf16[2,128,512]{2,1,0:T(8,128)(2,1)S(1)} %pad_maximum_fusion.3), channel_id=1, replica_groups=mesh['layer'=16,'dp'=2] {'dp'}, dimensions={1}, use_global_device_ids=true | all-gather | bytes 786432 | tf_op jit(solution)/shard_map/all_gather | solution.py:124
  201.6 4.1 %fusion.79 = f32[2,1024,512]{2,1,0:T(8,128)} fusion(bf16[2,256,512]{2,1,0:T(8,128)(2,1)S(1)} %all_gather.41, bf16[2,256,2048]{2,1,0:T(8,128)(2,1)} %all-gather.11.cloned.1.call-done, s32[]{:T(128)S(6)} %select_n.96), kind=kOutput, calls=%fused_computation.69 | convolution fusion | flops 536870912 | bytes 5767172 | tf_op jit(solution)/shard_map/ltf,ltd->lfd/dot_general | solution.py:128
  205.7 22.4 %all-gather.9.cloned.1.call-done = bf16[2,256,2048]{2,1,0:T(8,128)(2,1)} async-done(((bf16[2,128,2048]{2,1,0:T(8,128)(2,1)}), bf16[2,256,2048]{2,1,0:T(8,128)(2,1)}) %all-gather.9.cloned.1.call-update) | async-done | bytes 2097168 | tf_op jit(solution)/shard_map/all_gather | solution.py:122
  228.1 4.4 %fusion.100 = f32[2,256,2048]{2,1,0:T(8,128)} fusion(bf16[2,256,2048]{2,1,0:T(8,128)(2,1)} %all-gather.9.cloned.1.call-done, bf16[2,256,512]{2,1,0:T(8,128)(2,1)S(1)} %all_gather.38, s32[]{:T(128)S(6)} %select_n.95), kind=kOutput, calls=%fused_computation.97 | convolution fusion | flops 536870912 | bytes 6553604 | tf_op jit(solution)/shard_map/ltd,ltf->ldf/dot_general | solution.py:127
  (104 shorter events, 32.5 us)
Async XLA Ops:
  7.2 62.2 %all-gather.13.cloned.1.call-start = ((), (), s32[]{:S(2)}) async-start(), calls=%async_computation.2 | async-start | bytes 4456448 | tf_op jit(solution)/shard_map/all_gather | solution.py:12
  9.1 3.2 %copy-start.6 = (f32[1,512]{1,0:T(1,128)S(1)}, f32[1,512]{1,0:T(1,128)}, u32[]{:S(2)}) copy-start(f32[1,512]{1,0:T(1,128)} %param.15) | copy-start | bytes 6148
  9.1 3.2 %copy-start.3 = (f32[1,128,512]{2,1,0:T(8,128)S(1)}, f32[1,128,512]{2,1,0:T(8,128)}, u32[]{:S(2)}) copy-start(f32[1,128,512]{2,1,0:T(8,128)} %param.10) | copy-start | bytes 786436
  16.1 137.6 %all-gather.15.cloned.1.call-start = ((), (), s32[]{:S(2)}) async-start(), calls=%async_computation.3 | async-start | bytes 4456448 | tf_op jit(solution)/shard_map/all_gather | solution.py:12
  88.5 2.9 %copy-start.7 = (bf16[2,2048,512]{2,1,0:T(8,128)(2,1)S(1)}, bf16[2,2048,512]{2,1,0:T(8,128)(2,1)}, u32[]{:S(2)}) copy-start(bf16[2,2048,512]{2,1,0:T(8,128)(2,1)} %param.14) | copy-start | bytes 12582916
  88.6 14.0 %copy-start = (f32[128,512]{1,0:T(8,128)}, f32[128,512]{1,0:T(8,128)S(1)}, u32[]{:S(2)}) copy-start(f32[128,512]{1,0:T(8,128)S(1)} %get-tuple-element.291) | copy-start | bytes 786436
  91.4 2.2 copy-start.1
  91.4 2.7 %copy-start.4 = (f32[1,128,512]{2,1,0:T(8,128)S(1)}, f32[1,128,512]{2,1,0:T(8,128)}, u32[]{:S(2)}) copy-start(f32[1,128,512]{2,1,0:T(8,128)} %param.11) | copy-start | bytes 786436
  104.5 97.1 %all-gather.11.cloned.1.call-start = ((), (), s32[]{:S(2)}) async-start(), calls=%async_computation.1 | async-start | bytes 3145728 | tf_op jit(solution)/shard_map/all_gather | solution.py:123
  125.4 102.8 %all-gather.9.cloned.1.call-start = ((), (), s32[]{:S(2)}) async-start(), calls=%async_computation | async-start | bytes 3145728 | tf_op jit(solution)/shard_map/all_gather | solution.py:122
  173.0 3.9 %copy-start.5 = (f32[128,512]{1,0:T(8,128)}, f32[128,512]{1,0:T(8,128)S(1)}, u32[]{:S(2)}) copy-start(f32[128,512]{1,0:T(8,128)S(1)} %get-tuple-element.289) | copy-start | bytes 786436
  173.0 2.9 %copy-start.2 = (bf16[2,512,2048]{2,1,0:T(8,128)(2,1)S(1)}, bf16[2,512,2048]{2,1,0:T(8,128)(2,1)}, u32[]{:S(2)}) copy-start(bf16[2,512,2048]{2,1,0:T(8,128)(2,1)} %param.13) | copy-start | bytes 12582916
  175.9 2.2 copy-start.8
Sparse Core Ops, SparseCore 0:
  16.2 53.0 all-gather.12
  104.6 48.9 all-gather.14
  155.8 35.1 all-gather.10
  192.9 35.1 all-gather.8
where the time goes:
time: 240 us; the launch traced here: 239 us
  waiting for transfers between devices  80.6 us (34%)
  blocking collectives  63.9 us (27%)
  other arithmetic  43.3 us (18%)
  matrix products  31.5 us (13%)
  between operations  14 us (6%)
  local copies, waits for them, and re-layouts  4.58 us (2%)
    all_gather x2, waiting for transfers between devices, carried_in(): everything = jax.tree.map(lambda part: lax.all_gather(part, axis), x)  58.1 us
    all_gather x2, blocking collectives, carried_in(): everything = jax.tree.map(lambda part: lax.all_gather(part, axis), x)  42.4 us
    select_n x32, other arithmetic, step(): return jax.tree.map(lambda a, b: jnp.where(reached, a, b), new, before)  37.1 us
    all_gather x1, waiting for transfers between devices, shards(): piece_pre = lax.all_gather(pre_all, 'dp', axis=1, tiled=True)  22.4 us
    all_gather x1, blocking collectives, shards(): piece_normed = lax.all_gather(normed_all, 'dp', axis=1, tiled=True)  12.6 us
    dot_general x3, matrix products, layer_backward(): jnp.dot(pre_grad, up_matrix.T, preferred_element_type=jnp.float32)  9.26 us
    all_gather x1, blocking collectives, shards(): piece_out = lax.all_gather(out_all, 'dp', axis=1, tiled=True)  8.79 us
    dot_general x3, matrix products, layer_forward(): jnp.dot(hidden, down_matrix, preferred_element_type=jnp.float32)  7.55 us
  transfers between devices with their start and end apart: 4, of which 3 were waited for; matrix products, arithmetic and copies ran while one was open for 13% of the time, Pallas kernels for 0%

commit v1 on v0

--- a/solution.py
+++ b/solution.py
@@ -119,8 +119,11 @@
     width_share = w_up.shape[1] // group
     hidden_share = w_up.shape[2] // group
     piece_normed = lax.all_gather(normed_all, "dp", axis=1, tiled=True)
-    piece_pre = lax.all_gather(pre_all, "dp", axis=1, tiled=True)
-    piece_hidden = lax.all_gather(hidden_all, "dp", axis=1, tiled=True)
+    piece_pre, piece_hidden = jnp.split(
+        lax.all_gather(jnp.concatenate([pre_all, hidden_all], axis=0), "dp", axis=1, tiled=True),
+        [pre_all.shape[0]],
+        axis=0,
+    )
     piece_out = lax.all_gather(out_all, "dp", axis=1, tiled=True)
     normed_cols = lax.dynamic_slice_in_dim(piece_normed, member * width_share, width_share, 2)
     hidden_cols = lax.dynamic_slice_in_dim(piece_hidden, member * hidden_share, hidden_share, 2)

time: 240 us -> 270 us (1.12)
  local copies, waits for them, and re-layouts: 4.58 us -> 18.9 us
  waiting for transfers between devices: 80.6 us -> 94.8 us
  matrix products: 31.5 us -> 28.1 us
    all_gather x2 -> x1, waiting for transfers between devices: 22.4 us -> 36.9 us  [shards(): lax.all_gather(jnp.concatenate([pre_all, hidden_all], axis=0), 'dp', axis...]
    dynamic_slice x32, local copies, waits for them, and re-layouts: 0.31 us -> 11.8 us  [step(): new = combine(before, jax.tree.map(lambda part: part[at], everything))]
    all_gather x1, blocking collectives: 8.79 us -> 14.9 us  [shards(): piece_out = lax.all_gather(out_all, 'dp', axis=1, tiled=True)]
    all_gather x1, blocking collectives: 12.6 us -> 9.12 us  [shards(): piece_normed = lax.all_gather(normed_all, 'dp', axis=1, tiled=True)]
  transfers between devices with their start and end apart: 4 -> 3, of which waited for: 3 -> 3; matrix products, arithmetic and copies ran while one was open for 13% -> 1% of each run, Pallas kernels for 0% -> 0%
where the time goes in v1:
time: 270 us; the launch traced here: 268 us
  waiting for transfers between devices  94.8 us (35%)
  blocking collectives  66.5 us (25%)
  other arithmetic  44.4 us (16%)
  matrix products  28.1 us (10%)
  local copies, waits for them, and re-layouts  18.9 us (7%)
  between operations  14.1 us (5%)
    all_gather x2, waiting for transfers between devices, carried_in(): everything = jax.tree.map(lambda part: lax.all_gather(part, axis), x)  57.9 us
    all_gather x2, blocking collectives, carried_in(): everything = jax.tree.map(lambda part: lax.all_gather(part, axis), x)  42.4 us
    select_n x32, other arithmetic, step(): return jax.tree.map(lambda a, b: jnp.where(reached, a, b), new, before)  36.9 us
    all_gather x1, waiting for transfers between devices, shards(): lax.all_gather(jnp.concatenate([pre_all, hidden_all], axis=0), 'dp', axis...  36.9 us
    all_gather x1, blocking collectives, shards(): piece_out = lax.all_gather(out_all, 'dp', axis=1, tiled=True)  14.9 us
    dynamic_slice x32, local copies, waits for them, and re-layouts, step(): new = combine(before, jax.tree.map(lambda part: part[at], everything))  11.8 us
    all_gather x1, blocking collectives, shards(): piece_normed = lax.all_gather(normed_all, 'dp', axis=1, tiled=True)  9.12 us
    dot_general x3, matrix products, layer_backward(): jnp.dot(pre_grad, up_matrix.T, preferred_element_type=jnp.float32)  8.57 us
  transfers between devices with their start and end apart: 3, of which 3 were waited for; matrix products, arithmetic and copies ran while one was open for 1% of the time, Pallas kernels for 0%

profile of v1, /device:TPU:0, one launch (start us, length us, event | category | flops | bytes accessed | tf_op | source)
XLA Modules:
  0.0 267.8 jit_solution(12830621050831289323)
XLA Ops:
  9.1 3.2 %multiply_reduce_fusion.5 = (f32[128]{0:T(128)S(1)}, f32[128,512]{1,0:T(8,128)S(1)}) fusion(bf16[2,2048,512]{2,1,0:T(8,128)(2,1)} %param.14, bf16[2,512,2048]{2,1,0:T(8,128)(2,1)} %param.13, f32[1,128,512]{2,1,0:T(8,128)} %param.10, f32[512]{0:T(512)S(1)} %bitcast.177, f32[128]{0:T(128)S(1)} %add_rsqrt_fusion.3), kind=kOutput, calls=%fused_computation.108 | convolution fusion | flops 538640256 | bytes 4983808 | tf_op jit(solution)/shard_map/dot_general | solution.py:36
  12.3 3.7 %fusion.78 = f32[128,512]{1,0:T(8,128)} fusion(f32[128,512]{1,0:T(8,128)S(1)} %get-tuple-element.301, bf16[2,2048,512]{2,1,0:T(8,128)(2,1)} %param.14, bf16[2,512,2048]{2,1,0:T(8,128)(2,1)} %param.13, f32[1,128,512]{2,1,0:T(8,128)S(1)} %copy-done.5, f32[512]{0:T(512)S(1)} %bitcast.183, f32[512]{0:T(512)S(1)} %bitcast.172, f32[128]{0:T(128)S(1)} %add_rsqrt_fusion.2), kind=kOutput, calls=%fused_computation.69 | convolution fusion | flops 538640384 | bytes 5247488 | tf_op jit(solution)/shard_map/dot_general | solution.py:36
  16.1 23.3 %all-gather.2 = f32[16,1,512]{2,1,0:T(1,128)S(1)} all-gather(f32[1,1,512]{2,1,0:T(1,128)S(1)} %bitcast.184), channel_id=1, replica_groups=mesh['layer'=16,'dp'=2] {'layer'}, dimensions={0}, use_global_device_ids=true | all-gather | bytes 34816 | tf_op jit(solution)/shard_map/all_gather | solution.py:12
  39.5 29.9 %all-gather.10.cloned.1.call-done = f32[2048,512]{1,0:T(8,128)} async-done(((f32[128,512]{1,0:T(8,128)}), f32[2048,512]{1,0:T(8,128)}) %all-gather.10.cloned.1.call-update) | async-done | bytes 4194320 | tf_op jit(solution)/shard_map/all_gather | solution.py:12
  69.3 19.1 %while.30 = (s32[]{:T(128)}, f32[128,512]{1,0:T(8,128)S(1)}, s32[]{:T(128)}, f32[16,512]{1,0:T(8,128)S(1)}, f32[16,128,512]{2,1,0:T(8,128)}, /*index=5*/s32[]{:T(128)}, s32[]{:T(128)}) while((s32[]{:T(128)}, f32[128,512]{1,0:T(8,128)S(1)}, s32[]{:T(128)}, f32[16,512]{1,0:T(8,128)S(1)}, f32[16,128,512]{2,1,0:T(8,128)}, ...), condition=%wide.region_3.4_spmd.clone, body=%wide.region_2.3_spmd.clone.sunk | while | flops 262148 | bytes 792689 | solution.py:23
  70.5 1.2 fusion.150
  71.7 1.2 fusion.150
  72.9 1.2 fusion.150
  75.3 1.2 fusion.150
  76.5 1.2 fusion.150
  77.7 1.2 fusion.150
  78.9 1.2 fusion.150
  80.1 1.2 fusion.150
  81.3 1.2 fusion.150
  82.5 1.2 fusion.150
  89.1 2.5 fusion.33
  92.3 1.5 copy-done.2
  94.3 3.9 %multiply_reduce_fusion.2 = (f32[128]{0:T(128)S(1)}, f32[128,512]{1,0:T(8,128)S(1)}) fusion(f32[128,512]{1,0:T(8,128)S(1)} %get-tuple-element.303, f32[128]{0:T(128)S(1)} %add_rsqrt_fusion, f32[512]{0:T(512)S(1)} %bitcast.174, bf16[2,512,2048]{2,1,0:T(8,128)(2,1)} %param.13, bf16[2,2048,512]{2,1,0:T(8,128)(2,1)} %param.14, f32[128,2048]{1,0:T(8,128)S(1)} %fusion.21, ...), kind=kOutput, calls=%fused_computation.101 | convolution fusion | flops 539623296 | bytes 6032384 | tf_op jit(solution)/shard_map/dot_general | solution.py:50
  98.8 3.8 %fusion.51 = f32[128,512]{1,0:T(8,128)S(1)} fusion(bf16[2,512,2048]{2,1,0:T(8,128)(2,1)} %param.13, bf16[2,2048,512]{2,1,0:T(8,128)(2,1)} %param.14, f32[128,2048]{1,0:T(8,128)S(1)} %fusion.33, f32[512]{0:T(512)S(1)} %bitcast.179, f32[1,128,512]{2,1,0:T(8,128)S(1)} %copy-done.6, f32[128,512]{1,0:T(8,128)S(1)} %get-tuple-element.305, ...), kind=kOutput, calls=%fused_computation.60 | convolution fusion | flops 539754496 | bytes 6294528 | tf_op jit(solution)/shard_map/dot_general | solution.py:50
  103.5 1.6 fusion.134
  105.1 19.1 %all-gather.3 = f32[16,1,512]{2,1,0:T(1,128)S(1)} all-gather(f32[1,1,512]{2,1,0:T(1,128)S(1)} %bitcast.182), channel_id=1, replica_groups=mesh['layer'=16,'dp'=2] {'layer'}, dimensions={0}, use_global_device_ids=true | all-gather | bytes 34816 | tf_op jit(solution)/shard_map/all_gather | solution.py:12
  124.9 1.4 fusion.99
  126.2 28.0 %all-gather.12.cloned.1.call-done = f32[2048,512]{1,0:T(8,128)} async-done(((f32[128,512]{1,0:T(8,128)}), f32[2048,512]{1,0:T(8,128)}) %all-gather.12.cloned.1.call-update) | async-done | bytes 4194320 | tf_op jit(solution)/shard_map/all_gather | solution.py:12
  154.2 30.4 %while.31 = (s32[]{:T(128)}, f32[128,512]{1,0:T(8,128)S(1)}, s32[]{:T(128)}, f32[16,512]{1,0:T(8,128)}, f32[16,128,512]{2,1,0:T(8,128)}, /*index=5*/s32[]{:T(128)}, s32[]{:T(128)}, s32[]{:T(128)}, s32[]{:T(128)}) while((s32[]{:T(128)}, f32[128,512]{1,0:T(8,128)S(1)}, s32[]{:T(128)}, f32[16,512]{1,0:T(8,128)}, ...), condition=%wide.region_9.10_spmd.clone, body=%wide.region_8.9_spmd.clone.sunk | while | flops 262152 | bytes 792751 | solution.py:23
  185.3 2.6 fusion.8
  191.5 1.6 pad_maximum_fusion
  193.1 9.1 %all_gather.35 = bf16[2,256,512]{2,1,0:T(8,128)(2,1)S(1)} all-gather(bf16[2,128,512]{2,1,0:T(8,128)(2,1)S(1)} %pad_maximum_fusion.1), channel_id=1, replica_groups=mesh['layer'=16,'dp'=2] {'dp'}, dimensions={1}, use_global_device_ids=true | all-gather | bytes 786432 | tf_op jit(solution)/shard_map/all_gather | solution.py:121
  202.3 14.9 %all_gather.37 = bf16[2,256,512]{2,1,0:T(8,128)(2,1)S(1)} all-gather(bf16[2,128,512]{2,1,0:T(8,128)(2,1)S(1)} %pad_maximum_fusion.2), channel_id=1, replica_groups=mesh['layer'=16,'dp'=2] {'dp'}, dimensions={1}, use_global_device_ids=true | all-gather | bytes 786432 | tf_op jit(solution)/shard_map/all_gather | solution.py:127
  217.2 36.9 %all-gather.8.cloned.1.call-done = bf16[4,256,2048]{2,1,0:T(8,128)(2,1)} async-done(((bf16[4,128,2048]{2,1,0:T(8,128)(2,1)}), bf16[4,256,2048]{2,1,0:T(8,128)(2,1)}) %all-gather.8.cloned.1.call-update) | async-done | bytes 4194320 | tf_op jit(solution)/shard_map/all_gather | solution.py:123
  254.1 1.6 slice-done
  255.7 2.8 %fusion.81 = f32[2,1024,512]{2,1,0:T(8,128)} fusion(bf16[2,256,512]{2,1,0:T(8,128)(2,1)S(1)} %all_gather.37, bf16[2,256,2048]{2,1,0:T(8,128)(2,1)S(1)} %slice-done, s32[]{:T(128)S(6)} %select_n.96), kind=kOutput, calls=%fused_computation.70 | convolution fusion | flops 536870912 | bytes 5767172 | tf_op jit(solution)/shard_map/ltf,ltd->lfd/dot_general | solution.py:131
  258.5 2.8 %fusion.11 = f32[2,256,2048]{2,1,0:T(8,128)} fusion(bf16[4,256,2048]{2,1,0:T(8,128)(2,1)S(1)} %copy-done, bf16[2,256,512]{2,1,0:T(8,128)(2,1)S(1)} %all_gather.35, s32[]{:T(128)S(6)} %select_n.95), kind=kOutput, calls=%fused_computation.19 | convolution fusion | flops 536870912 | bytes 6553604 | tf_op jit(solution)/shard_map/ltd,ltf->ldf/dot_general | solution.py:130
  (116 shorter events, 47.2 us)
Async XLA Ops:
  7.2 62.2 %all-gather.10.cloned.1.call-start = ((), (), s32[]{:S(2)}) async-start(), calls=%async_computation.1 | async-start | bytes 4456448 | tf_op jit(solution)/shard_map/all_gather | solution.py:12
  9.1 3.2 %copy-start.12 = (f32[1,512]{1,0:T(1,128)S(1)}, f32[1,512]{1,0:T(1,128)}, u32[]{:S(2)}) copy-start(f32[1,512]{1,0:T(1,128)} %param.15) | copy-start | bytes 6148
  9.1 3.3 %copy-start.5 = (f32[1,128,512]{2,1,0:T(8,128)S(1)}, f32[1,128,512]{2,1,0:T(8,128)}, u32[]{:S(2)}) copy-start(f32[1,128,512]{2,1,0:T(8,128)} %param.10) | copy-start | bytes 786436
  16.1 138.1 %all-gather.12.cloned.1.call-start = ((), (), s32[]{:S(2)}) async-start(), calls=%async_computation.2 | async-start | bytes 4456448 | tf_op jit(solution)/shard_map/all_gather | solution.py:12
  88.5 3.2 %copy-start.14 = (bf16[2,2048,512]{2,1,0:T(8,128)(2,1)S(1)}, bf16[2,2048,512]{2,1,0:T(8,128)(2,1)}, u32[]{:S(2)}) copy-start(bf16[2,2048,512]{2,1,0:T(8,128)(2,1)} %param.14) | copy-start | bytes 12582916
  88.6 14.9 %copy-start.1 = (f32[128,512]{1,0:T(8,128)}, f32[128,512]{1,0:T(8,128)S(1)}, u32[]{:S(2)}) copy-start(f32[128,512]{1,0:T(8,128)S(1)} %get-tuple-element.291) | copy-start | bytes 786436
  88.6 0.5 copy-start.11
  91.7 2.2 copy-start.2
  91.7 2.7 copy-start.6
  98.2 0.6 copy-start.13
  105.1 79.6 %copy-start.7 = (f32[1,128,512]{2,1,0:T(8,128)S(1)}, f32[1,128,512]{2,1,0:T(8,128)}, u32[]{:S(2)}) copy-start(f32[1,128,512]{2,1,0:T(8,128)} %param.11) | copy-start | bytes 786436
  105.1 149.0 %all-gather.8.cloned.1.call-start = ((), (), s32[]{:S(2)}) async-start(), calls=%async_computation | async-start | bytes 6291456 | tf_op jit(solution)/shard_map/all_gather | solution.py:123
  185.3 3.8 %copy-start.8 = (f32[128,512]{1,0:T(8,128)}, f32[128,512]{1,0:T(8,128)S(1)}, u32[]{:S(2)}) copy-start(f32[128,512]{1,0:T(8,128)S(1)} %get-tuple-element.289) | copy-start | bytes 786436
  185.3 2.9 %copy-start.3 = (bf16[2,512,2048]{2,1,0:T(8,128)(2,1)S(1)}, bf16[2,512,2048]{2,1,0:T(8,128)(2,1)}, u32[]{:S(2)}) copy-start(bf16[2,512,2048]{2,1,0:T(8,128)(2,1)} %param.13) | copy-start | bytes 12582916
  188.2 2.2 copy-start.15
  190.4 1.0 copy-start.4
  191.3 1.7 copy-start.10
  191.3 10.9 %copy-start.9 = (bf16[1,128,512]{2,1,0:T(8,128)(2,1)S(1)}, bf16[1,128,512]{2,1,0:T(8,128)(2,1)}, u32[]{:S(2)}) copy-start(bf16[1,128,512]{2,1,0:T(8,128)(2,1)} %get-tuple-element.288) | copy-start | bytes 393220
  254.1 1.6 slice-start
  254.1 4.4 %copy-start = (bf16[4,256,2048]{2,1,0:T(8,128)(2,1)S(1)}, bf16[4,256,2048]{2,1,0:T(8,128)(2,1)}, u32[]{:S(2)}) copy-start(bf16[4,256,2048]{2,1,0:T(8,128)(2,1)} %all-gather.8.cloned.1.call-done) | copy-start | bytes 12582916
Sparse Core Ops, SparseCore 0:
  16.2 53.0 all-gather.9
  105.2 48.9 all-gather.11
  193.2 60.8 all-gather.7
